TPU v7x, 128 devices: a whole 4x4x4 slice. The times are simulated.
128 devices in a mesh: wide: 32 (over z, x, core), narrow: 4 (over y).
Axes of the slice: x: 4, y: 4, z: 4, core: 2. Of those that a mesh axis runs over, the one named last changes fastest.
Arguments:
- amps: bfloat16 [256, 128, 128], P(('wide', 'narrow')), may hold values from -4 to 4
- resp: bfloat16 [256, 128, 128], P(('wide', 'narrow')), may hold values from -4 to 4
- trans: bfloat16 [256, 512, 128], P(('wide', 'narrow')), may hold values from -0.375 to 0.375
- ints: bfloat16 [256, 128, 128], P(('wide', 'narrow')), may hold values from -6 to 6
- energies: float32 [256, 128], P(('wide', 'narrow')), may hold values from 0.5 to 4
- couple: float32 [256, 48], P(('wide', 'narrow')), may hold values from -1 to 1
- readers: int32 [256, 48], P(('wide', 'narrow')), may hold values from 0 to 63, as said below
- domains: int32 [256, 4], replicated, may hold values from 0 to 7, as said below
- integrals: bfloat16 [1024, 512], P(None, 'narrow'), may hold values from -0.01171875 to 0.01171875
Outputs:
- new_amps: float32 [256, 128, 128], P(('wide', 'narrow'))
- new_resp: float32 [256, 128, 128], P(('wide', 'narrow'))
- response: float32 [1024, 512], P('wide', 'narrow')
Inputs may be any that keep to these rules, and one draw needn't show every extreme that they name: `readers`: each row lists 48 different positions among the 64 pairs of the same narrow index. `domains`: each row lists 4 different function blocks.
All inputs are finite; a program needn't handle non-finite values.
Results may differ from a plain program's by a relative error of at most 0.015.
Values may be sent and summed in bfloat16 or wider, within the bound.
A program may use at most 64 MiB of HBM per device.

v0:
```python
import jax
import jax.numpy as jnp
from jax import lax
from jax.sharding import PartitionSpec as P

NPNO = 128
BLK = 128
NFB = 8


def reader_terms(own_q, own_dom, their_q, their_dom, their_amps):
    blocks = own_q.shape[0]
    reader_count = their_q.shape[0]
    matches = (own_dom[None, :, None] == their_dom[:, None, :]).astype(jnp.bfloat16)
    split_q = their_q.reshape(reader_count, blocks, BLK, NPNO)
    shifted = jnp.einsum(
        "sab,sbfp->safp", matches, split_q, preferred_element_type=jnp.float32
    ).astype(jnp.bfloat16)
    intersection = jnp.einsum(
        "afp,safq->spq", own_q, shifted, preferred_element_type=jnp.float32
    ).astype(jnp.bfloat16)
    halfway = jnp.einsum(
        "spq,sqc->spc", intersection, their_amps, preferred_element_type=jnp.float32
    ).astype(jnp.bfloat16)
    halfway = halfway.reshape(reader_count, NPNO, 2, NPNO)
    return jnp.einsum("spkc,sqc->skpq", halfway, intersection, preferred_element_type=jnp.float32)


def per_device(amps, resp, trans, ints, energies, couple, readers, domains, integrals):
    wide_size = lax.axis_size("wide")
    narrow_size = lax.axis_size("narrow")
    wide_pos = lax.axis_index("wide")
    narrow_pos = lax.axis_index("narrow")
    pairs_here = amps.shape[0]
    dom_blk = trans.shape[1] // BLK
    grid = domains.reshape(wide_size, narrow_size, pairs_here, dom_blk)
    dom_row = lax.dynamic_index_in_dim(grid, narrow_pos, axis=1, keepdims=False).reshape(
        wide_size * pairs_here, dom_blk
    )
    own_dom = lax.dynamic_slice_in_dim(
        domains, (wide_pos * narrow_size + narrow_pos) * pairs_here, pairs_here, 0
    )
    own_q = trans.reshape(pairs_here, dom_blk, BLK, NPNO)
    pair_amps = jnp.concatenate([amps, resp], axis=2)
    gathered_q, gathered_amps = (
        lax.all_gather(trans, "wide", axis=0, tiled=True),
        lax.all_gather(pair_amps, "wide", axis=0, tiled=True),
    )
    collected = []
    for member in range(pairs_here):
        picks = readers[member]
        contrib = reader_terms(
            own_q[member], own_dom[member], gathered_q[picks], dom_row[picks], gathered_amps[picks]
        )
        collected.append(jnp.einsum("s,skpq->kpq", couple[member], contrib))
    coupled = jnp.stack(collected)
    amps_f = amps.astype(jnp.float32)
    resp_f = resp.astype(jnp.float32)
    denominator = energies[:, :, None] + energies[:, None, :]
    new_amps = (
        amps_f
        - 0.5 * (ints.astype(jnp.float32) + denominator * amps_f + coupled[:, 0]) / denominator
    )
    new_resp = resp_f - 0.5 * (amps_f + denominator * resp_f + coupled[:, 1]) / denominator
    amps_b = new_amps.astype(jnp.bfloat16)
    resp_b = new_resp.astype(jnp.bfloat16)
    weights = 0.5 * (
        jnp.einsum("gpc,gqc->gpq", amps_b, resp_b, preferred_element_type=jnp.float32)
        + jnp.einsum("gpc,gqc->gpq", resp_b, amps_b, preferred_element_type=jnp.float32)
    )
    weights = weights.astype(jnp.bfloat16)
    place = (jnp.arange(NFB, dtype=jnp.int32)[None, :, None] == own_dom[:, None, :]).astype(
        jnp.bfloat16
    )
    full_q = jnp.einsum("gnd,gdfp->gnfp", place, own_q, preferred_element_type=jnp.float32)
    full_q = full_q.astype(jnp.bfloat16).reshape(pairs_here, NFB * BLK, NPNO)
    left = jnp.einsum("gmp,gpq->gmq", full_q, weights, preferred_element_type=jnp.float32).astype(
        jnp.bfloat16
    )
    share = lax.psum_scatter(
        jnp.einsum("gmq,gnq->mn", left, full_q, preferred_element_type=jnp.float32),
        ("wide", "narrow"),
        scatter_dimension=0,
        tiled=True,
    )
    panel = lax.all_gather(share, "narrow", axis=0, tiled=True)
    response = jnp.dot(panel, integrals.astype(jnp.float32), precision=lax.Precision.HIGHEST)
    return (new_amps, new_resp, response)


def solution(mesh):
    in_specs = (
        P(("wide", "narrow"), None, None),
        P(("wide", "narrow"), None, None),
        P(("wide", "narrow"), None, None),
        P(("wide", "narrow"), None, None),
        P(("wide", "narrow"), None),
        P(("wide", "narrow"), None),
        P(("wide", "narrow"), None),
        P(),
        P(None, "narrow"),
    )
    out_specs = (
        P(("wide", "narrow"), None, None),
        P(("wide", "narrow"), None, None),
        P("wide", "narrow"),
    )
    return jax.shard_map(
        per_device, mesh=mesh, in_specs=in_specs, out_specs=out_specs, check_vma=False
    )
```

profile of v0, /device:TPU:1, one launch (start us, length us, event | category | flops | bytes accessed | tf_op | source)
XLA Modules:
  0.0 835.2 jit_solution(1243034435495024713)
XLA Ops:
  7.2 0.0 copy-start
  7.2 0.0 copy-start.4
  7.2 0.0 all-gather.5.cloned.1.call-start
  7.2 1.6 pad_maximum_fusion.1
  8.8 0.0 all-gather.5.cloned.1.call-update
  8.9 0.0 all-gather.3.cloned.1.call-start
  8.9 0.7 all-gather.3.cloned.1.call-update
  9.6 0.0 reduce-scatter.2.cloned.1.call-start
  9.7 0.8 copy.23
  10.5 0.8 fusion.59
  11.3 1.2 gather_fusion
  12.5 1.2 gather_fusion.3
  13.6 0.8 constant_dynamic-slice_fusion.1
  14.4 0.1 copy.34
  14.5 1.4 convolution_convert_fusion.1
  15.9 0.9 copy.36
  16.8 0.2 slice_reduce_fusion.1
  17.0 0.0 copy-done.4
  17.0 0.7 fusion.67
  17.7 42.9 %all-gather.5.cloned.1.call-done = bf16[64,128,256]{2,1,0:T(8,128)(2,1)} async-done(((bf16[2,128,256]{2,1,0:T(8,128)(2,1)}), bf16[64,128,256]{2,1,0:T(8,128)(2,1)}) %all-gather.5.cloned.1.call-update) | async-done | bytes 4194320 | tf_op jit(solution)/shard_map/all_gather | solution.py:47
  60.6 2.9 gather_fusion.2
  63.6 4.7 gather_fusion.5
  68.3 46.8 %all-gather.3.cloned.1.call-done = bf16[64,512,128]{2,1,0:T(8,128)(2,1)} async-done(((bf16[2,512,128]{2,1,0:T(8,128)(2,1)}), bf16[64,512,128]{2,1,0:T(8,128)(2,1)}) %all-gather.3.cloned.1.call-update) | async-done | bytes 8388624 | tf_op jit(solution)/shard_map/all_gather | solution.py:46
  115.1 8.4 %gather_fusion.1 = bf16[48,512,128]{2,1,0:T(8,128)(2,1)} fusion(bf16[64,512,128]{2,1,0:T(8,128)(2,1)} %all-gather.3.cloned.1.call-done, s32[1024]{0:T(1024)S(1)} %get-tuple-element.12), kind=kCustom, calls=%fused_computation.1 | custom fusion | bytes 12583104 | tf_op jit(solution)/shard_map/gather | solution.py:53
  123.5 0.0 copy-start.9
  123.5 8.8 %fusion.8 = bf16[48,4,128,128]{3,1,2,0:T(4,128)(2,1)S(1)} fusion(bf16[48,4,128,128]{3,2,1,0:T(8,128)(2,1)} %bitcast.119, s32[48,4]{1,0:T(8,128)} %gather_fusion, s32[4]{0:T(128)S(1)} %get-tuple-element.3), kind=kOutput, calls=%fused_computation.14 | convolution fusion | flops 28312320 | bytes 12583696 | tf_op jit(solution)/shard_map/sab,sbfp->safp/dot_general | solution.py:16
  132.3 0.0 copy-done.9
  132.3 1.9 bitcast_convert_fusion.1
  134.2 1.0 convert_bitcast_fusion.1
  135.3 2.8 fusion.20
  138.0 3.7 copy.41
  141.7 8.4 %gather_fusion.4 = bf16[48,512,128]{2,1,0:T(8,128)(2,1)} fusion(bf16[64,512,128]{2,1,0:T(8,128)(2,1)} %all-gather.3.cloned.1.call-done, s32[1024]{0:T(1024)S(1)} %get-tuple-element.11), kind=kCustom, calls=%fused_computation.4 | custom fusion | bytes 12583104 | tf_op jit(solution)/shard_map/gather | solution.py:53
  150.1 8.8 %fusion.11 = bf16[48,4,128,128]{3,1,2,0:T(4,128)(2,1)S(1)} fusion(bf16[48,4,128,128]{3,2,1,0:T(8,128)(2,1)} %bitcast.118, s32[48,4]{1,0:T(8,128)} %gather_fusion.3, s32[4]{0:T(128)S(1)} %get-tuple-element.4), kind=kOutput, calls=%fused_computation.15 | convolution fusion | flops 28312320 | bytes 12583696 | tf_op jit(solution)/shard_map/sab,sbfp->safp/dot_general | solution.py:16
  158.9 0.0 copy-start.2
  158.9 1.9 bitcast_convert_fusion
  160.8 0.0 copy-done.2
  160.8 1.0 convert_bitcast_fusion
  161.9 2.7 fusion.23
  164.5 5.0 copy.48
  169.5 0.0 copy-done.11
  169.5 0.0 copy-start.8
  169.5 0.0 copy-start.10
  169.5 0.0 copy-start.12
  169.5 0.5 fusion.63
  170.1 1.3 copy-done.1
  171.4 0.5 fusion.61
  171.9 0.0 copy-done.7
  171.9 0.0 copy-done.8
  171.9 0.0 copy-done.10
  171.9 0.0 copy-done.12
  171.9 0.1 convert_subtract_fusion.1
  172.1 0.0 copy-start.5
  172.1 0.0 copy-start.6
  172.1 0.2 fusion.52
  172.3 0.2 fusion.33
  172.5 0.0 copy-done.3
  172.5 2.8 convolution_bitcast_fusion
  175.3 0.0 reduce-scatter.2.cloned.1.call-update
  175.3 0.0 copy-done.5
  175.3 0.0 copy-done.6
  175.3 642.8 %reduce-scatter.2.cloned.1.call-done = f32[8,1024]{1,0:T(8,128)} async-done(((f32[1024,1024]{1,0:T(8,128)}), f32[8,1024]{1,0:T(8,128)}) %reduce-scatter.2.cloned.1.call-update) | async-done | bytes 32784 | tf_op jit(solution)/shard_map/reduce_scatter | solution.py:80
  818.1 9.7 %all_gather.11 = f32[32,1024]{1,0:T(8,128)S(1)} all-gather(f32[8,1024]{1,0:T(8,128)} %reduce-scatter.2.cloned.1.call-done), channel_id=1, replica_groups=mesh['wide'=32,'narrow'=4] {'narrow'}, dimensions={0}, use_global_device_ids=true | all-gather | bytes 163840 | tf_op jit(solution)/shard_map/all_gather | solution.py:86
  827.8 0.0 copy-done
  827.8 0.8 fusion.68
  (6 shorter events, 0.0 us)
Async XLA Ops:
  7.2 820.6 %copy-start = (bf16[1024,128]{1,0:T(8,128)(2,1)S(1)}, bf16[1024,128]{1,0:T(8,128)(2,1)}, u32[]{:S(2)}) copy-start(bf16[1024,128]{1,0:T(8,128)(2,1)} %param.17) | copy-start | bytes 786436
  7.2 9.8 %copy-start.4 = (bf16[2,512,128]{2,1,0:T(8,128)(2,1)S(1)}, bf16[2,512,128]{2,1,0:T(8,128)(2,1)}, u32[]{:S(2)}) copy-start(bf16[2,512,128]{2,1,0:T(8,128)(2,1)} %param.11) | copy-start | bytes 786436
  7.2 53.4 %all-gather.5.cloned.1.call-start = ((), (), s32[]{:S(2)}) async-start(), calls=%async_computation.2 | async-start | bytes 4325376 | tf_op jit(solution)/shard_map/all_gather | solution.py:47
  8.9 106.2 %all-gather.3.cloned.1.call-start = ((), (), s32[]{:S(2)}) async-start(), calls=%async_computation.1 | async-start | bytes 8650752 | tf_op jit(solution)/shard_map/all_gather | solution.py:46
  9.6 808.5 %reduce-scatter.2.cloned.1.call-start = ((), (), s32[]{:S(2)}) async-start(), calls=%async_computation.3 | async-start | bytes 4227072 | tf_op jit(solution)/shard_map/reduce_scatter | solution.py:80
  123.5 8.8 %copy-start.9 = (bf16[1,512,128]{2,1,0:T(8,128)(2,1)S(1)}, bf16[1,512,128]{2,1,0:T(8,128)(2,1)}, u32[]{:S(2)}) copy-start(bf16[1,512,128]{2,1,0:T(8,128)(2,1)} %get-tuple-element.7) | copy-start | bytes 393220
  158.9 1.9 copy-start.2
  164.5 5.0 copy-start.11
  169.5 1.9 copy-start.1
  169.5 2.4 copy-start.7
  169.5 2.4 copy-start.8
  169.5 2.4 copy-start.10
  169.5 2.4 copy-start.12
  171.4 1.1 copy-start.3
  172.1 3.2 copy-start.5
  172.1 3.2 copy-start.6
Sparse Core Ops, SparseCore 0:
  10.8 49.7 all-gather.4
  62.9 52.1 all-gather.2
  175.4 642.6 reduce-scatter.1
where the time goes:
time: 846 us; the launch traced here: 835 us
  waiting for transfers between devices  733 us (87%)
  local copies, waits for them, and re-layouts  40.3 us (5%)
  matrix products  35.3 us (4%)
  between operations  14 us (2%)
  blocking collectives  9.71 us (1%)
    reduce_scatter x1, waiting for transfers between devices, per_device(): lax.psum_scatter(jnp.einsum('gmq,gnq->mn', left, full_q, preferred_elemen...  643 us
    all_gather x1, waiting for transfers between devices, per_device(): lax.all_gather(trans, 'wide', axis=0, tiled=True)  46.8 us
    all_gather x1, waiting for transfers between devices, per_device(): lax.all_gather(pair_amps, 'wide', axis=0, tiled=True)  42.9 us
    dot_general x2, matrix products, reader_terms(): jnp.einsum('sab,sbfp->safp', matches, split_q, preferred_element_type=jnp...  17.6 us
  transfers between devices with their start and end apart: 3, of which 3 were waited for; matrix products, arithmetic and copies ran while one was open for 2% of the time, Pallas kernels for 0%

commit v1 on v0

v1 whole, which is shorter than its diff:
```python
import jax
import jax.numpy as jnp
from jax import lax
from jax.experimental import pallas as pl
from jax.experimental.pallas import tpu as pltpu
from jax.sharding import PartitionSpec as P

MESH = pl.DeviceIdType.MESH
F32 = jnp.float32
BF16 = jnp.bfloat16
RING = 4
PIECES = 32
ROWS = 256

QH, TH, ZH, QG, CG, RG, XA, RS, WB, PC = 0, 16, 32, 48, 56, 60, 64, 68, 74, 82
N_RECV = PC + PIECES
N_SEND = 112
PIECE_SEND = 80


def dot(a, b):
    return jnp.dot(a, b, preferred_element_type=F32)


def dot_nt(a, b):
    return lax.dot_general(a, b, (((1,), (1,)), ((), ())), preferred_element_type=F32)


def dot_tn(a, b):
    return lax.dot_general(a, b, (((0,), (0,)), ((), ())), preferred_element_type=F32)


def kernel(
    amps, resp, trans, ints, energies, couple, readers, domains, integrals,
    out_t, out_z, out_r,
    qh, th, zh, qg, at, sall, hall, xall, yall, fsel, lall, wb, coef, cg, rg,
    rs_send, rs_recv, obuf, rbuf, local_sem, send_sem, recv_sem,
):
    wide = lax.axis_index("wide")
    y = lax.axis_index("narrow")
    c = lax.rem(wide, 2)
    x = lax.rem(wide // 2, RING)
    z = wide // (2 * RING)

    def device(dz=0, dx=0, dc=0, dy=0):
        zz, xx = lax.rem(z + dz, RING), lax.rem(x + dx, RING)
        return ((zz * RING + xx) * 2 + lax.rem(c + dc, 2), lax.rem(y + dy, RING))

    sends = []

    def send(src, dst, recv, where):
        copy = pltpu.make_async_remote_copy(
            src_ref=src, dst_ref=dst, send_sem=send_sem.at[len(sends)],
            recv_sem=recv_sem.at[recv], device_id=where, device_id_type=MESH,
        )
        sends.append(copy)
        copy.start()

    def arrive(ref, recv):
        pltpu.make_async_remote_copy(
            src_ref=ref, dst_ref=ref, send_sem=send_sem.at[0],
            recv_sem=recv_sem.at[recv], device_id=device(dc=1), device_id_type=MESH,
        ).wait_recv()

    up_z, down_z = device(dz=1), device(dz=3)
    up_x, down_x = device(dx=1), device(dx=3)
    sibling = device(dc=1)

    locals_ = []
    for p in range(2):
        for src, dst in (
            (trans.at[p], qh.at[p]), (amps.at[p], th.at[p]), (resp.at[p], zh.at[p]),
            (trans.at[p], qg.at[p]),
        ):
            locals_.append((src, dst))
    locals_.append((couple, cg.at[0]))
    locals_.append((readers, rg.at[0]))
    locals_.append((integrals, xall.at[0]))
    copies = [
        pltpu.make_async_copy(src, dst, local_sem.at[i]) for i, (src, dst) in enumerate(locals_)
    ]
    for copy in copies:
        copy.start()

    barrier = pltpu.get_barrier_semaphore()

    @pl.loop(1, PIECES)
    def _(i):
        where = device(dx=lax.rem(i // 2, RING), dc=lax.rem(i, 2), dy=i // 8)
        pl.semaphore_signal(barrier, inc=1, device_id=where, device_id_type=MESH)

    for where in (up_z, down_z):
        pl.semaphore_signal(barrier, inc=1, device_id=where, device_id_type=MESH)
    for copy in copies:
        copy.wait()
    pl.semaphore_wait(barrier, PIECES + 1)

    def send_pair(s, to, where):
        send(qh.at[s], qh.at[to], QH + to, where)
        send(th.at[s], th.at[to], TH + to, where)
        send(zh.at[s], zh.at[to], ZH + to, where)

    def arrive_pair(s):
        arrive(qh.at[s], QH + s)
        arrive(th.at[s], TH + s)
        arrive(zh.at[s], ZH + s)

    def send_g(s, to, where):
        send(qg.at[s], qg.at[to], QG + to, where)

    def arrive_g(s):
        arrive(qg.at[s], QG + s)

    send_pair(0, 4, up_z)
    send_pair(1, 5, down_z)
    send_g(0, 6, up_x)
    send_g(1, 3, down_x)
    send_pair(0, 2, sibling)
    send_pair(1, 3, sibling)
    send_pair(1, 8, up_z)
    send_pair(0, 9, down_z)
    send_g(1, 7, up_x)
    send_g(0, 2, down_x)
    for d in range(1, RING):
        send(cg.at[0], cg.at[RING - d], CG + RING - d, device(dx=d))
        send(rg.at[0], rg.at[RING - d], RG + RING - d, device(dx=d))
    for d in (1, 3, 2):
        send(xall.at[0], xall.at[RING - d], XA + RING - d, device(dy=d))

    def domain_of(index):
        return [domains[index, a] for a in range(4)]

    def build_at(k):
        index = (
            ((z * RING + lax.rem(x + k // 2, RING)) * 2 + c) * RING + y
        ) * 2 + lax.rem(k, 2)
        own = domain_of(index)
        turned = [jnp.transpose(qg[k, a * 128:(a + 1) * 128, :]) for a in range(4)]
        zero = jnp.zeros((128, 128), BF16)
        rows = pl.ds(pl.multiple_of(k * 128, 128), 128)
        for block in range(8):
            value = zero
            for a in range(4):
                value = lax.select(own[a] == block, turned[a], value)
            at[block, rows, :] = value

    def each(low, high, body):
        def step(i, carry):
            body(i)
            return carry
        lax.fori_loop(low, high, step, 0)

    def place(s):
        group, inner = s // 4, lax.rem(s, 4)
        flip, i = inner // 2, lax.rem(inner, 2)
        near = jnp.where(i == 0, 3, 1)
        dz = jnp.where(group == 0, 0, jnp.where(group == 3, 2, near))
        pair = jnp.where(group == 2, 1 - i, i)
        return lax.rem(z + dz, RING), lax.rem(c + flip, 2), pair

    def index_of(s):
        zz, cc, pair = place(s)
        return (((zz * RING + x) * 2 + cc) * RING + y) * 2 + pair

    each(0, 2, build_at)
    arrive_g(6)
    send_g(6, 4, up_x)
    arrive_g(3)
    send_g(3, 5, down_x)
    each(3, 4, build_at)
    each(6, 7, build_at)
    for slot in (4, 5):
        arrive_pair(slot)
        send_pair(slot, 12 if slot == 4 else 13, up_z if slot == 4 else down_z)
        send_pair(slot, slot + 2, sibling)
    arrive_g(2)
    each(2, 3, build_at)
    arrive_g(7)
    each(7, 8, build_at)

    for d in range(1, RING):
        arrive(cg.at[d], CG + d)
        arrive(rg.at[d], RG + d)
    slots = lax.broadcasted_iota(jnp.int32, (16, 48), 0)
    zz, cc, pair = place(slots)
    position = ((zz * RING + x) * 2 + cc) * 2 + pair
    for k in range(8):
        row = rg[k // 2, k % 2:k % 2 + 1, :]
        weight = cg[k // 2, k % 2:k % 2 + 1, :]
        picked = jnp.where(position == row, weight, 0.0)
        coef[k] = jnp.broadcast_to(jnp.sum(picked, axis=1, keepdims=True), (16, 128))

    arrive_g(4)
    each(4, 5, build_at)
    arrive_g(5)
    each(5, 6, build_at)

    def tile(s):
        theirs = domain_of(index_of(s))
        columns = pl.ds(pl.multiple_of(s * 128, 128), 128)
        both = jnp.concatenate([th[s], zh[s]], axis=1)
        for low in range(0, 1024, ROWS):
            left = jnp.concatenate(
                [at[theirs[b], low:low + ROWS, :] for b in range(4)], axis=1
            )
            inter = dot(left, qh[s]).astype(BF16)
            half = dot(inter, both)
            for i in range(ROWS // 128):
                k = low // 128 + i
                rows = slice(i * 128, (i + 1) * 128)
                weight = coef[k, pl.ds(s, 1), :]
                sall[k, :, columns] = inter[rows]
                hall[k, 0:128, columns] = (half[rows, 0:128] * weight).astype(BF16)
                hall[k, 128:256, columns] = (half[rows, 128:256] * weight).astype(BF16)

    for slot in (2, 3):
        arrive_pair(slot)
    each(0, 4, tile)
    for slot in (6, 7):
        arrive_pair(slot)
    each(4, 8, tile)
    for slot in (8, 9):
        arrive_pair(slot)
        send_pair(slot, slot + 2, sibling)
    for slot in (12, 13):
        arrive_pair(slot)
        send_pair(slot, slot + 2, sibling)
    for slot in (10, 11):
        arrive_pair(slot)
    each(8, 12, tile)
    for slot in (14, 15):
        arrive_pair(slot)
    each(12, 16, tile)

    def coupled(k):
        return dot_nt(hall[k], sall[k])

    def pass_on(i, value, where):
        rs_send[i] = value.astype(BF16)
        send(rs_send.at[i], rs_recv.at[i], RS + i, where)

    pass_on(0, coupled(4), up_x)
    pass_on(1, coupled(5), down_x)
    pass_on(2, coupled(3), up_x)
    pass_on(3, coupled(6), down_x)
    part0, part1 = coupled(2), coupled(7)
    arrive(rs_recv.at[0], RS + 0)
    pass_on(4, part0 + rs_recv[0].astype(F32), up_x)
    arrive(rs_recv.at[1], RS + 1)
    pass_on(5, part1 + rs_recv[1].astype(F32), down_x)
    for d in range(1, RING):
        arrive(xall.at[d], XA + d)

    def own_slot(j):
        return (j // 2) * 4 + lax.rem(j, 2)

    def columns_of(j):
        s = own_slot(j)
        theirs = domain_of(index_of(s))
        wide_rows = [
            jnp.concatenate([xall[d, theirs[b]] for d in range(RING)], axis=1) for b in range(4)
        ]
        rows = pl.ds(pl.multiple_of(j * 128, 128), 128)
        yall[rows, :] = dot_tn(qh[s], jnp.concatenate(wide_rows, axis=0)).astype(BF16)
        zero = jnp.zeros((128, 128), BF16)
        for i in range(2):
            value = zero
            for b in range(4):
                value = lax.select(
                    theirs[b] == 2 * z + i, qh[s, b * 128:(b + 1) * 128, :], value
                )
            fsel[j, i * 128:(i + 1) * 128, :] = value

    each(0, 8, columns_of)

    own = [coupled(0), coupled(1)]
    for p in range(2):
        near, far = ((3, 4), (2, 5))[p]
        arrive(rs_recv.at[near], RS + near)
        arrive(rs_recv.at[far], RS + far)
        total = own[p] + rs_recv[near].astype(F32) + rs_recv[far].astype(F32)
        across = jnp.broadcast_to(energies[p:p + 1, :], (128, 128))
        denom = across + jnp.transpose(across)
        amp = th[p].astype(F32)
        res = zh[p].astype(F32)
        new_t = amp - 0.5 * (ints[p].astype(F32) + denom * amp + total[0:128]) / denom
        new_z = res - 0.5 * (amp + denom * res + total[128:256]) / denom
        out_t[p] = new_t
        out_z[p] = new_z
        product = dot_nt(new_t.astype(BF16), new_z.astype(BF16))
        wb[p] = (0.5 * (product + jnp.transpose(product))).astype(BF16)

    def send_w(s, to, where):
        send(wb.at[s], wb.at[to], WB + to, where)

    send_w(0, 2, up_z)
    send_w(1, 3, down_z)
    send_w(1, 4, up_z)
    send_w(0, 5, down_z)
    arrive(wb.at[2], WB + 2)
    send_w(2, 6, up_z)
    arrive(wb.at[3], WB + 3)
    send_w(3, 7, down_z)

    def left_of(j):
        columns = pl.ds(pl.multiple_of(j * 128, 128), 128)
        lall[:, columns] = dot(fsel[j], wb[j]).astype(BF16)

    each(0, 4, left_of)
    for j in (4, 5):
        arrive(wb.at[j], WB + j)
    each(4, 6, left_of)
    for j in (6, 7):
        arrive(wb.at[j], WB + j)
    each(6, 8, left_of)
    partial = dot(lall[...], yall[...])
    for d in range(RING):
        for i in range(8):
            obuf[d, i] = partial[i * 32:(i + 1) * 32, d * 128:(d + 1) * 128].astype(BF16)

    def piece(i):
        dx, dc, dy = lax.rem(i // 2, RING), lax.rem(i, 2), i // 8
        return pltpu.make_async_remote_copy(
            src_ref=obuf.at[dy, lax.rem(x + dx, RING) * 2 + lax.rem(c + dc, 2)],
            dst_ref=rbuf.at[i], send_sem=send_sem.at[PIECE_SEND + i],
            recv_sem=recv_sem.at[PC + i], device_id=device(dx=dx, dc=dc, dy=dy),
            device_id_type=MESH,
        )

    each(1, PIECES, lambda i: piece(i).start())
    for copy in sends:
        copy.wait_send()
    out_r[...] = obuf[0, x * 2 + c].astype(F32)

    def take(i):
        piece(i).wait_recv()
        out_r[...] += rbuf[i].astype(F32)

    each(1, PIECES, take)
    each(1, PIECES, lambda i: piece(i).wait_send())


def per_device(amps, resp, trans, ints, energies, couple, readers, domains, integrals):
    vmem = pl.BlockSpec(memory_space=pltpu.VMEM)
    anywhere = pl.BlockSpec(memory_space=pl.ANY)
    dma = pltpu.SemaphoreType.DMA
    return pl.pallas_call(
        kernel,
        out_shape=(
            jax.ShapeDtypeStruct((2, 128, 128), F32),
            jax.ShapeDtypeStruct((2, 128, 128), F32),
            jax.ShapeDtypeStruct((32, 128), F32),
        ),
        in_specs=[
            anywhere, anywhere, anywhere, vmem, vmem, vmem, vmem,
            pl.BlockSpec(memory_space=pltpu.SMEM), anywhere,
        ],
        out_specs=(vmem, vmem, vmem),
        scratch_shapes=[
            pltpu.VMEM((16, 512, 128), BF16),
            pltpu.VMEM((16, 128, 128), BF16),
            pltpu.VMEM((16, 128, 128), BF16),
            pltpu.VMEM((8, 512, 128), BF16),
            pltpu.VMEM((8, 1024, 128), BF16),
            pltpu.VMEM((8, 128, 2048), BF16),
            pltpu.VMEM((8, 256, 2048), BF16),
            pltpu.VMEM((4, 8, 128, 128), BF16),
            pltpu.VMEM((1024, 512), BF16),
            pltpu.VMEM((8, 256, 128), BF16),
            pltpu.VMEM((256, 1024), BF16),
            pltpu.VMEM((8, 128, 128), BF16),
            pltpu.VMEM((8, 16, 128), F32),
            pltpu.VMEM((4, 2, 48), F32),
            pltpu.VMEM((4, 2, 48), jnp.int32),
            pltpu.VMEM((6, 256, 128), BF16),
            pltpu.VMEM((6, 256, 128), BF16),
            pltpu.VMEM((4, 8, 32, 128), BF16),
            pltpu.VMEM((PIECES, 32, 128), BF16),
            dma((16,)), dma((N_SEND,)), dma((N_RECV,)),
        ],
        compiler_params=pltpu.CompilerParams(
            collective_id=0, has_side_effects=True, vmem_limit_bytes=60 * 1024 * 1024
        ),
    )(amps, resp, trans, ints, energies, couple, readers, domains, integrals.reshape(8, 128, 128))


def solution(mesh):
    pairs3 = P(("wide", "narrow"), None, None)
    pairs2 = P(("wide", "narrow"), None)
    return jax.shard_map(
        per_device,
        mesh=mesh,
        in_specs=(
            pairs3, pairs3, pairs3, pairs3, pairs2, pairs2, pairs2, P(), P(None, "narrow"),
        ),
        out_specs=(pairs3, pairs3, P("wide", "narrow")),
        check_vma=False,
    )
```

time: 846 us -> 71.8 us (0.08); the launches traced: 835 us -> 71.5 us
  waiting for transfers between devices: 733 us -> 0 us
  Pallas kernels: 0 us -> 66.4 us
  local copies, waits for them, and re-layouts: 40.3 us -> 4.41 us
  matrix products: 35.3 us -> 0 us
  between operations: 14 us -> 0.65 us
  blocking collectives: 9.71 us -> 0 us
    reduce_scatter x1 -> x0, waiting for transfers between devices: 643 us -> none  [per_device(): lax.psum_scatter(jnp.einsum('gmq,gnq->mn', left, full_q, preferred_elemen...]
    all_gather x2 -> x0, waiting for transfers between devices: 89.8 us -> none  [the longest x1 46.8 us: per_device(): lax.all_gather(trans, 'wide', axis=0, tiled=True)]
    pallas_call x0 -> x1, Pallas kernels: none -> 66.4 us  [per_device(): pl.pallas_call(kernel, out_shape=(jax.ShapeDtypeStruct((2, 128, 128), F32...]
    dot_general x15 -> x0, matrix products: 35.3 us -> none  [the longest x2 17.6 us: reader_terms(): jnp.einsum('sab,sbfp->safp', matches, split_q, preferred_element_type=jnp...]
    gather x6 -> x0, local copies, waits for them, and re-layouts: 26.8 us -> none  [the longest x2 16.8 us: per_device(): gathered_q[picks]]
    all_gather x1 -> x0, blocking collectives: 9.71 us -> none  [per_device(): panel = lax.all_gather(share, 'narrow', axis=0, tiled=True)]
    transpose x2 -> x0, local copies, waits for them, and re-layouts: 8.64 us -> none  [reader_terms(): jnp.einsum('spkc,sqc->skpq', halfway, intersection, preferred_element_typ...]
  transfers between devices with their start and end apart: 3 -> 0, of which waited for: 3 -> 0; matrix products, arithmetic and copies ran while one was open for 2% -> 0% of each run, Pallas kernels for 0% -> 0%
where the time goes in v1:
time: 71.8 us; the launch traced here: 71.5 us
  Pallas kernels  66.4 us (92%)
  local copies, waits for them, and re-layouts  4.41 us (6%)
    pallas_call x1, Pallas kernels, per_device(): pl.pallas_call(kernel, out_shape=(jax.ShapeDtypeStruct((2, 128, 128), F32...  66.4 us
    unnamed x8, local copies, waits for them, and re-layouts  4.41 us

profile of v1, /device:TPU:1, one launch (start us, length us, event | category | flops | bytes accessed | tf_op | source)
XLA Modules:
  0.0 71.5 jit_solution(6250372314866539002)
XLA Ops:
  0.6 1.5 %copy.12.domains = s32[256,4]{1,0:T(8,128)} copy(s32[256,4]{0,1:T(4,128)} %param.16) | data formatting | bytes 8192 | tf_op args[7]
  2.1 66.4 %shard_map.112 = (f32[2,128,128]{2,1,0:T(8,128)}, f32[2,128,128]{2,1,0:T(8,128)}, f32[32,128]{1,0:T(8,128)}) custom-call(bf16[2,128,128]{2,1,0:T(8,128)(2,1)} %amps.1, bf16[2,128,128]{2,1,0:T(8,128)(2,1)} %resp.1, bf16[2,512,128]{2,1,0:T(8,128)(2,1)} %trans.1, bf16[2,128,128]{2,1,0:T(8,128)(2,1)} %ints.1, f32[2,128]{1,0:T(2,128)} %energies.1, ...), custom_call_target="tpu_custom_call" | custom-call | tf_op jit(solution)/shard_map/pallas_call | solution.py:347
  68.5 0.0 copy-start
  68.6 1.6 %copy.16 = f32[2,128,128]{2,1,0:T(8,128)} copy(f32[2,128,128]{2,1,0:T(8,128)} %get-tuple-element.6) | data formatting | bytes 262144
  70.2 0.0 copy-done
  70.2 0.0 copy-start.1
  70.2 0.7 copy.17
  70.8 0.1 copy-done.1
  70.9 0.6 copy.18
Async XLA Ops:
  68.5 1.6 %copy-start = (f32[2,128,128]{2,1,0:T(8,128)S(1)}, f32[2,128,128]{2,1,0:T(8,128)}, u32[]{:S(2)}) copy-start(f32[2,128,128]{2,1,0:T(8,128)} %get-tuple-element.7) | copy-start | bytes 393220
  70.2 0.7 %copy-start.1 = (f32[32,128]{1,0:T(8,128)S(1)}, f32[32,128]{1,0:T(8,128)}, u32[]{:S(2)}) copy-start(f32[32,128]{1,0:T(8,128)} %get-tuple-element.8) | copy-start | bytes 49156

commit v2 on v1

v2 whole, which is shorter than its diff:
```python
import jax
import jax.numpy as jnp
from jax import lax
from jax.experimental import pallas as pl
from jax.experimental.pallas import tpu as pltpu
from jax.sharding import PartitionSpec as P

MESH = pl.DeviceIdType.MESH
F32 = jnp.float32
BF16 = jnp.bfloat16
RING = 4
PIECES = 32
HALF = 512
G_PLACE = ((0, 0), (0, 1), (3, 0), (1, 1), (3, 1), (1, 0), (2, 0), (2, 1))

HB, QG, CG, RG, XA, RS, WB, PC = 0, 16, 24, 28, 32, 40, 46, 54
N_RECV = PC + PIECES
N_SEND = 112
PIECE_SEND = 80


def dot(a, b):
    return jnp.dot(a, b, preferred_element_type=F32)


def dot_nt(a, b):
    return lax.dot_general(a, b, (((1,), (1,)), ((), ())), preferred_element_type=F32)


def dot_tn(a, b):
    return lax.dot_general(a, b, (((0,), (0,)), ((), ())), preferred_element_type=F32)


def each(low, high, body):
    def step(i, carry):
        body(i)
        return carry
    lax.fori_loop(low, high, step, 0)


def kernel(
    amps, resp, trans, ints, energies, couple, readers, domains, integrals,
    out_t, out_z, out_r,
    hb, qg, at, sall, hall, xall, yall, fsel, lall, wb, coef, cg, rg, dom, ex, en,
    base, scale, new, rs_send, rs_recv, obuf, rbuf, rsum,
    local_sem, send_sem, recv_sem, known,
):
    wide = lax.axis_index("wide")
    y = lax.axis_index("narrow")
    c = lax.rem(wide, 2)
    x = lax.rem(wide // 2, RING)
    z = wide // (2 * RING)

    def device(dz=0, dx=0, dc=0, dy=0):
        zz, xx = lax.rem(z + dz, RING), lax.rem(x + dx, RING)
        return ((zz * RING + xx) * 2 + lax.rem(c + dc, 2), lax.rem(y + dy, RING))

    up_z, down_z = device(dz=1), device(dz=3)
    up_x, down_x = device(dx=1), device(dx=3)
    up_y, down_y = device(dy=1), device(dy=3)
    sibling = device(dc=1)

    def tell(sem, *where):
        for one in where:
            pl.semaphore_signal(sem, inc=1, device_id=one, device_id_type=MESH)

    barrier = pltpu.get_barrier_semaphore()
    tell(barrier, up_z, down_z, up_x, down_x, sibling, up_y, down_y)

    moves = []
    for p in range(2):
        moves += [
            (trans.at[p], hb.at[p, 0:512]), (amps.at[p], hb.at[p, 512:640]),
            (resp.at[p], hb.at[p, 640:768]),
        ]
    moves += [
        (couple, cg.at[0]), (readers, rg.at[0]), (integrals, xall.at[0]), (domains, dom),
        (ints, ex), (energies, en),
    ]
    copies = [
        pltpu.make_async_copy(src, dst, local_sem.at[i]) for i, (src, dst) in enumerate(moves)
    ]
    for copy in copies:
        copy.start()
    for copy in copies:
        copy.wait()
    pl.semaphore_wait(barrier, 7)

    sends = []

    def send(src, dst, recv, where):
        copy = pltpu.make_async_remote_copy(
            src_ref=src, dst_ref=dst, send_sem=send_sem.at[len(sends)],
            recv_sem=recv_sem.at[recv], device_id=where, device_id_type=MESH,
        )
        sends.append(copy)
        copy.start()

    def arrive(ref, recv):
        pltpu.make_async_remote_copy(
            src_ref=ref, dst_ref=ref, send_sem=send_sem.at[0],
            recv_sem=recv_sem.at[recv], device_id=sibling, device_id_type=MESH,
        ).wait_recv()

    def send_pair(s, to, where):
        send(hb.at[s], hb.at[to], HB + to, where)

    def arrive_pair(*slots):
        for s in slots:
            arrive(hb.at[s], HB + s)

    def send_g(src, to, where):
        send(src, qg.at[to], QG + to, where)

    def arrive_g(*slots):
        for s in slots:
            arrive(qg.at[s], QG + s)

    def send_x(d, half, to, where):
        rows = slice(half * 4, half * 4 + 4)
        send(xall.at[d, rows], xall.at[to, rows], XA + to * 2 + half, where)

    def arrive_x(d, half):
        arrive(xall.at[d, half * 4:half * 4 + 4], XA + d * 2 + half)

    send_pair(0, 4, up_z)
    send_pair(1, 5, down_z)
    send_g(hb.at[0, 0:512], 2, up_x)
    send_g(hb.at[1, 0:512], 3, down_x)
    send_pair(0, 2, sibling)
    send_pair(1, 3, sibling)
    send_pair(1, 8, up_z)
    send_pair(0, 9, down_z)
    send_g(hb.at[1, 0:512], 4, up_x)
    send_g(hb.at[0, 0:512], 5, down_x)
    for src, base_sem in ((cg, CG), (rg, RG)):
        send(src.at[0], src.at[3], base_sem + 3, up_x)
        send(src.at[0], src.at[1], base_sem + 1, down_x)
    send_x(0, 0, 3, up_y)
    send_x(0, 1, 1, down_y)
    send_x(0, 1, 3, up_y)
    send_x(0, 0, 1, down_y)

    def domain_of(index):
        return [dom[a, index] for a in range(4)]

    zero = jnp.zeros((128, 128), BF16)

    def pair_of_g(k):
        return G_PLACE[k]

    def build_at(k):
        dx, pair = pair_of_g(k)
        own = domain_of((((z * RING + lax.rem(x + dx, RING)) * 2 + c) * RING + y) * 2 + pair)
        source = hb if k < 2 else qg
        turned = [jnp.transpose(source[k, a * 128:(a + 1) * 128, :]) for a in range(4)]
        for block in range(8):
            value = zero
            for a in range(4):
                value = lax.select(own[a] == block, turned[a], value)
            at[block, k * 128:(k + 1) * 128, :] = value

    def place(s):
        group, inner = s // 4, lax.rem(s, 4)
        flip, i = inner // 2, lax.rem(inner, 2)
        near = jnp.where(i == 0, 3, 1)
        dz = jnp.where(group == 0, 0, jnp.where(group == 3, 2, near))
        pair = jnp.where(group == 2, 1 - i, i)
        return lax.rem(z + dz, RING), lax.rem(c + flip, 2), pair

    def index_of(s):
        zz, cc, pair = place(s)
        return (((zz * RING + x) * 2 + cc) * RING + y) * 2 + pair

    def tile(i, low):
        pair = (2 * i, 2 * i + 1)
        inters = []
        for s in pair:
            theirs = domain_of(index_of(s))
            left = jnp.concatenate([at[theirs[b], low:low + HALF, :] for b in range(4)], axis=1)
            inters.append(dot(left, hb[s, 0:512, :]).astype(BF16))
        for s, inter in zip(pair, inters):
            columns = pl.ds(pl.multiple_of(s * 128, 128), 128)
            both = jnp.concatenate([hb[s, 512:640, :], hb[s, 640:768, :]], axis=1)
            half = dot(inter, both)
            for j in range(HALF // 128):
                k = low // 128 + j
                rows = slice(j * 128, (j + 1) * 128)
                weight = coef[k, pl.ds(s, 1), :]
                sall[k, :, columns] = inter[rows]
                hall[k, 0:128, columns] = (half[rows, 0:128] * weight).astype(BF16)
                hall[k, 128:256, columns] = (half[rows, 128:256] * weight).astype(BF16)

    def coefficients(ks):
        slots = lax.broadcasted_iota(jnp.int32, (16, 48), 0)
        zz, cc, pair = place(slots)
        position = ((zz * RING + x) * 2 + cc) * 2 + pair
        for k in ks:
            dx, p = pair_of_g(k)
            row = rg[dx, p:p + 1, :]
            weight = cg[dx, p:p + 1, :]
            picked = jnp.where(position == row, weight, 0.0)
            coef[k] = jnp.broadcast_to(jnp.sum(picked, axis=1, keepdims=True), (16, 128))

    build_at(0)
    build_at(1)
    for p in range(2):
        across = jnp.broadcast_to(en[p:p + 1, :], (128, 128))
        denom = across + jnp.transpose(across)
        amp = hb[p, 512:640, :].astype(F32)
        res = hb[p, 640:768, :].astype(F32)
        scale[p] = 0.5 / denom
        base[p, 0] = amp - 0.5 * (ex[p].astype(F32) + denom * amp) / denom
        base[p, 1] = res - 0.5 * (amp + denom * res) / denom
    for src, base_sem in ((cg, CG), (rg, RG)):
        arrive(src.at[3], base_sem + 3)
        send(src.at[3], src.at[2], base_sem + 2, up_x)
        arrive(src.at[1], base_sem + 1)
    tell(known.at[0], up_x, down_x)
    coefficients((0, 1, 2, 3, 4, 5))
    arrive_g(2)
    send_g(qg.at[2], 6, up_x)
    arrive_g(3)
    send_g(qg.at[3], 7, down_x)
    build_at(2)
    build_at(3)
    arrive_pair(2, 3)
    each(0, 2, lambda i: tile(i, 0))
    arrive_x(3, 0)
    send_x(3, 0, 2, up_y)
    arrive_x(1, 1)
    send_x(1, 1, 2, down_y)
    arrive_pair(4)
    send_pair(4, 12, up_z)
    send_pair(4, 6, sibling)
    arrive_pair(5)
    send_pair(5, 13, down_z)
    send_pair(5, 7, sibling)
    for src, base_sem in ((cg, CG), (rg, RG)):
        arrive(src.at[2], base_sem + 2)
    coefficients((6, 7))
    arrive_g(4, 5)
    build_at(4)
    build_at(5)
    arrive_pair(6, 7)
    each(2, 4, lambda i: tile(i, 0))
    pl.semaphore_wait(known.at[0], 2)
    tell(known.at[1], sibling)
    arrive_g(6, 7)
    build_at(6)
    build_at(7)
    arrive_pair(8)
    send_pair(8, 10, sibling)
    arrive_pair(9)
    send_pair(9, 11, sibling)
    each(0, 4, lambda i: tile(i, HALF))
    arrive_pair(10, 11)

    def whole(i):
        tile(i, 0)
        tile(i, HALF)

    each(4, 6, whole)
    pl.semaphore_wait(known.at[1], 1)
    tell(known.at[2], up_y, down_y)
    arrive_pair(12)
    send_pair(12, 14, sibling)
    arrive_pair(13)
    send_pair(13, 15, sibling)
    each(6, 7, whole)
    arrive_pair(14, 15)
    each(7, 8, whole)

    def coupled(k):
        return dot_nt(hall[k], sall[k])

    def pass_on(i, value, where):
        rs_send[i] = value.astype(BF16)
        send(rs_send.at[i], rs_recv.at[i], RS + i, where)

    pass_on(0, coupled(6), up_x)
    pass_on(1, coupled(7), down_x)
    pass_on(2, coupled(3), up_x)
    pass_on(3, coupled(2), down_x)
    part0, part1 = coupled(5), coupled(4)
    arrive(rs_recv.at[0], RS + 0)
    pass_on(4, part0 + rs_recv[0].astype(F32), up_x)
    arrive(rs_recv.at[1], RS + 1)
    pass_on(5, part1 + rs_recv[1].astype(F32), down_x)
    pl.semaphore_wait(known.at[2], 2)
    tell(known.at[3], up_y, down_y)
    for d, half in ((3, 1), (1, 0), (2, 0), (2, 1)):
        arrive_x(d, half)

    def columns_of(j):
        s = (j // 2) * 4 + lax.rem(j, 2)
        theirs = domain_of(index_of(s))
        wide_rows = [
            jnp.concatenate([xall[d, theirs[b]] for d in range(RING)], axis=1) for b in range(4)
        ]
        rows = pl.ds(pl.multiple_of(j * 128, 128), 128)
        yall[rows, :] = dot_tn(hb[s, 0:512, :], jnp.concatenate(wide_rows, axis=0)).astype(BF16)
        for i in range(2):
            value = zero
            for b in range(4):
                value = lax.select(
                    theirs[b] == 2 * z + i, hb[s, b * 128:(b + 1) * 128, :], value
                )
            fsel[j, i * 128:(i + 1) * 128, :] = value

    each(0, 8, columns_of)
    own = [coupled(0), coupled(1)]
    for p in range(2):
        near, far = ((3, 4), (2, 5))[p]
        arrive(rs_recv.at[near], RS + near)
        arrive(rs_recv.at[far], RS + far)
        total = own[p] + rs_recv[near].astype(F32) + rs_recv[far].astype(F32)
        new_t = base[p, 0] - total[0:128] * scale[p]
        new_z = base[p, 1] - total[128:256] * scale[p]
        new[0, p] = new_t
        new[1, p] = new_z
        product = dot_nt(new_t.astype(BF16), new_z.astype(BF16))
        wb[p] = (0.5 * (product + jnp.transpose(product))).astype(BF16)

    def send_w(s, to, where):
        send(wb.at[s], wb.at[to], WB + to, where)

    send_w(0, 2, up_z)
    send_w(1, 3, down_z)
    send_w(1, 4, up_z)
    send_w(0, 5, down_z)
    outs = [
        pltpu.make_async_copy(new.at[0], out_t, local_sem.at[0]),
        pltpu.make_async_copy(new.at[1], out_z, local_sem.at[1]),
    ]
    for copy in outs:
        copy.start()
    pl.semaphore_wait(known.at[3], 2)

    def left_of(*js):
        for j in js:
            lall[:, j * 128:(j + 1) * 128] = dot(fsel[j], wb[j]).astype(BF16)

    left_of(0, 1)
    arrive(wb.at[2], WB + 2)
    send_w(2, 6, up_z)
    arrive(wb.at[3], WB + 3)
    send_w(3, 7, down_z)
    left_of(2, 3)
    for j in (4, 5):
        arrive(wb.at[j], WB + j)
    left_of(4, 5)
    early = dot(lall[:, 0:768], yall[0:768, :])
    for j in (6, 7):
        arrive(wb.at[j], WB + j)
    left_of(6, 7)

    def piece(i):
        dy, dx, dc = i // 8, (i // 2) % 4, i % 2
        return pltpu.make_async_remote_copy(
            src_ref=obuf.at[dy, lax.rem(x + dx, RING) * 2 + lax.rem(c + dc, 2)],
            dst_ref=rbuf.at[i], send_sem=send_sem.at[PIECE_SEND + i],
            recv_sem=recv_sem.at[PC + i], device_id=device(dx=dx, dc=dc, dy=dy),
            device_id_type=MESH,
        )

    pieces = [None] + [piece(i) for i in range(1, PIECES)]
    for dys in ((2, 3), (0, 1)):
        columns = slice(dys[0] * 128, dys[0] * 128 + 256)
        partial = early[:, columns] + dot(lall[:, 768:1024], yall[768:1024, columns])
        for d in dys:
            for i in range(8):
                block = partial[i * 32:(i + 1) * 32, (d - dys[0]) * 128:(d - dys[0] + 1) * 128]
                obuf[d, i] = block.astype(BF16)
        for d in dys:
            for i in (4, 5, 2, 3, 6, 7, 1, 0):
                if d * 8 + i:
                    pieces[d * 8 + i].start()
    for copy in sends:
        copy.wait_send()
    for copy in outs:
        copy.wait()
    total = obuf[0, x * 2 + c].astype(F32)
    for i in range(1, PIECES):
        pieces[i].wait_recv()
        total = total + rbuf[i].astype(F32)
    rsum[...] = total
    last = pltpu.make_async_copy(rsum, out_r, local_sem.at[2])
    last.start()
    for i in range(1, PIECES):
        pieces[i].wait_send()
    last.wait()


def per_device(amps, resp, trans, ints, energies, couple, readers, domains, integrals):
    anywhere = pl.BlockSpec(memory_space=pl.ANY)
    dma = pltpu.SemaphoreType.DMA
    return pl.pallas_call(
        kernel,
        out_shape=(
            jax.ShapeDtypeStruct((2, 128, 128), F32),
            jax.ShapeDtypeStruct((2, 128, 128), F32),
            jax.ShapeDtypeStruct((32, 128), F32),
        ),
        in_specs=[anywhere] * 9,
        out_specs=(anywhere,) * 3,
        scratch_shapes=[
            pltpu.VMEM((16, 768, 128), BF16),
            pltpu.VMEM((8, 512, 128), BF16),
            pltpu.VMEM((8, 1024, 128), BF16),
            pltpu.VMEM((8, 128, 2048), BF16),
            pltpu.VMEM((8, 256, 2048), BF16),
            pltpu.VMEM((4, 8, 128, 128), BF16),
            pltpu.VMEM((1024, 512), BF16),
            pltpu.VMEM((8, 256, 128), BF16),
            pltpu.VMEM((256, 1024), BF16),
            pltpu.VMEM((8, 128, 128), BF16),
            pltpu.VMEM((8, 16, 128), F32),
            pltpu.VMEM((4, 2, 48), F32),
            pltpu.VMEM((4, 2, 48), jnp.int32),
            pltpu.SMEM((4, 256), jnp.int32),
            pltpu.VMEM((2, 128, 128), BF16),
            pltpu.VMEM((2, 128), F32),
            pltpu.VMEM((2, 2, 128, 128), F32),
            pltpu.VMEM((2, 128, 128), F32),
            pltpu.VMEM((2, 2, 128, 128), F32),
            pltpu.VMEM((6, 256, 128), BF16),
            pltpu.VMEM((6, 256, 128), BF16),
            pltpu.VMEM((4, 8, 32, 128), BF16),
            pltpu.VMEM((PIECES, 32, 128), BF16),
            pltpu.VMEM((32, 128), F32),
            dma((16,)), dma((N_SEND,)), dma((N_RECV,)), pltpu.SemaphoreType.REGULAR((4,)),
        ],
        compiler_params=pltpu.CompilerParams(
            collective_id=0, has_side_effects=True, vmem_limit_bytes=60 * 1024 * 1024
        ),
    )(
        amps, resp, trans, ints, energies, couple, readers, domains.T,
        integrals.reshape(8, 128, 128),
    )


def solution(mesh):
    pairs3 = P(("wide", "narrow"), None, None)
    pairs2 = P(("wide", "narrow"), None)
    return jax.shard_map(
        per_device,
        mesh=mesh,
        in_specs=(
            pairs3, pairs3, pairs3, pairs3, pairs2, pairs2, pairs2, P(), P(None, "narrow"),
        ),
        out_specs=(pairs3, pairs3, P("wide", "narrow")),
        check_vma=False,
    )
```

time: 71.8 us -> 56.7 us (0.79)
  Pallas kernels: 66.4 us -> 52.9 us
  local copies, waits for them, and re-layouts: 4.41 us -> 2.93 us
    pallas_call x1, Pallas kernels: 66.4 us -> 52.9 us  [per_device(): pl.pallas_call(kernel, out_shape=(jax.ShapeDtypeStruct((2, 128, 128), F32...]
    unnamed x8 -> x7, local copies, waits for them, and re-layouts: 4.41 us -> 2.93 us
where the time goes in v2:
time: 56.7 us; the launch traced here: 56.5 us
  Pallas kernels  52.9 us (93%)
  local copies, waits for them, and re-layouts  2.93 us (5%)
  between operations  0.65 us (1%)
    pallas_call x1, Pallas kernels, per_device(): pl.pallas_call(kernel, out_shape=(jax.ShapeDtypeStruct((2, 128, 128), F32...  52.9 us
    unnamed x7, local copies, waits for them, and re-layouts  2.93 us

profile of v2, /device:TPU:1, one launch (start us, length us, event | category | flops | bytes accessed | tf_op | source)
XLA Modules:
  0.0 56.5 jit_solution(1334029967791155462)
XLA Ops:
  0.6 52.9 %shard_map.112 = (f32[2,128,128]{2,1,0:T(8,128)}, f32[2,128,128]{2,1,0:T(8,128)}, f32[32,128]{1,0:T(8,128)}) custom-call(bf16[2,128,128]{2,1,0:T(8,128)(2,1)} %amps.1, bf16[2,128,128]{2,1,0:T(8,128)(2,1)} %resp.1, bf16[2,512,128]{2,1,0:T(8,128)(2,1)} %trans.1, bf16[2,128,128]{2,1,0:T(8,128)(2,1)} %ints.1, f32[2,128]{1,0:T(2,128)} %energies.1, ...), custom_call_target="tpu_custom_call" | custom-call | tf_op jit(solution)/shard_map/pallas_call | solution.py:398
  53.5 0.0 copy-start
  53.5 1.6 %copy.15 = f32[2,128,128]{2,1,0:T(8,128)} copy(f32[2,128,128]{2,1,0:T(8,128)} %get-tuple-element.6) | data formatting | bytes 262144
  55.2 0.0 copy-done
  55.2 0.0 copy-start.1
  55.2 0.7 %copy.16 = f32[2,128,128]{2,1,0:T(8,128)} copy(f32[2,128,128]{2,1,0:T(8,128)S(1)} %copy-done) | data formatting | bytes 262144
  55.8 0.1 copy-done.1
  55.9 0.6 %copy.17 = f32[32,128]{1,0:T(8,128)} copy(f32[32,128]{1,0:T(8,128)S(1)} %copy-done.1) | data formatting | bytes 32768
Async XLA Ops:
  53.5 1.6 %copy-start = (f32[2,128,128]{2,1,0:T(8,128)S(1)}, f32[2,128,128]{2,1,0:T(8,128)}, u32[]{:S(2)}) copy-start(f32[2,128,128]{2,1,0:T(8,128)} %get-tuple-element.7) | copy-start | bytes 393220
  55.2 0.7 %copy-start.1 = (f32[32,128]{1,0:T(8,128)S(1)}, f32[32,128]{1,0:T(8,128)}, u32[]{:S(2)}) copy-start(f32[32,128]{1,0:T(8,128)} %get-tuple-element.8) | copy-start | bytes 49156

commit v3 on v2

--- a/solution.py
+++ b/solution.py
@@ -13,10 +13,10 @@
 HALF = 512
 G_PLACE = ((0, 0), (0, 1), (3, 0), (1, 1), (3, 1), (1, 0), (2, 0), (2, 1))
 
-HB, QG, CG, RG, XA, RS, WB, PC = 0, 16, 24, 28, 32, 40, 46, 54
+HB, HC, QG, CG, RG, XA, RS, WB, PC = 0, 16, 32, 40, 44, 48, 56, 62, 70
 N_RECV = PC + PIECES
-N_SEND = 112
-PIECE_SEND = 80
+N_SEND = 140
+PIECE_SEND = 104
 
 
 def dot(a, b):
@@ -42,7 +42,7 @@
     amps, resp, trans, ints, energies, couple, readers, domains, integrals,
     out_t, out_z, out_r,
     hb, qg, at, sall, hall, xall, yall, fsel, lall, wb, coef, cg, rg, dom, ex, en,
-    base, scale, new, rs_send, rs_recv, obuf, rbuf, rsum,
+    base, scale, rs_send, rs_recv, obuf, rbuf,
     local_sem, send_sem, recv_sem, known,
 ):
     wide = lax.axis_index("wide")
@@ -82,8 +82,6 @@
     ]
     for copy in copies:
         copy.start()
-    for copy in copies:
-        copy.wait()
     pl.semaphore_wait(barrier, 7)
 
     sends = []
@@ -109,6 +107,16 @@
         for s in slots:
             arrive(hb.at[s], HB + s)
 
+    PARTS = ((slice(0, 384), HB), (slice(384, 768), HC))
+
+    def send_part(s, part, to, where):
+        rows, sem = PARTS[part]
+        send(hb.at[s, rows], hb.at[to, rows], sem + to, where)
+
+    def arrive_part(s, part):
+        rows, sem = PARTS[part]
+        arrive(hb.at[s, rows], sem + s)
+
     def send_g(src, to, where):
         send(src, qg.at[to], QG + to, where)
 
@@ -123,23 +131,29 @@
     def arrive_x(d, half):
         arrive(xall.at[d, half * 4:half * 4 + 4], XA + d * 2 + half)
 
-    send_pair(0, 4, up_z)
-    send_pair(1, 5, down_z)
-    send_g(hb.at[0, 0:512], 2, up_x)
-    send_g(hb.at[1, 0:512], 3, down_x)
-    send_pair(0, 2, sibling)
-    send_pair(1, 3, sibling)
-    send_pair(1, 8, up_z)
-    send_pair(0, 9, down_z)
-    send_g(hb.at[1, 0:512], 4, up_x)
-    send_g(hb.at[0, 0:512], 5, down_x)
-    for src, base_sem in ((cg, CG), (rg, RG)):
-        send(src.at[0], src.at[3], base_sem + 3, up_x)
-        send(src.at[0], src.at[1], base_sem + 1, down_x)
-    send_x(0, 0, 3, up_y)
-    send_x(0, 1, 1, down_y)
-    send_x(0, 1, 3, up_y)
-    send_x(0, 0, 1, down_y)
+    def send_own(p, to, where):
+        send(trans.at[p], hb.at[to, 0:512], HB + to, where)
+        send(amps.at[p], hb.at[to, 512:640], HB + to, where)
+        send(resp.at[p], hb.at[to, 640:768], HB + to, where)
+
+    send_own(0, 4, up_z)
+    send_own(1, 5, down_z)
+    send_g(trans.at[0], 2, up_x)
+    send_g(trans.at[1], 3, down_x)
+    send_own(0, 2, sibling)
+    send_own(1, 3, sibling)
+    send_own(1, 8, up_z)
+    send_own(0, 9, down_z)
+    send_g(trans.at[1], 4, up_x)
+    send_g(trans.at[0], 5, down_x)
+    for src, dst, base_sem in ((couple, cg, CG), (readers, rg, RG)):
+        send(src, dst.at[3], base_sem + 3, up_x)
+        send(src, dst.at[1], base_sem + 1, down_x)
+    for half, to, where in ((0, 3, up_y), (1, 1, down_y), (1, 3, up_y), (0, 1, down_y)):
+        rows = slice(half * 4, half * 4 + 4)
+        send(integrals.at[rows], xall.at[to, rows], XA + to * 2 + half, where)
+    for copy in copies:
+        copy.wait()
 
     def domain_of(index):
         return [dom[a, index] for a in range(4)]
@@ -231,10 +245,12 @@
     arrive_x(1, 1)
     send_x(1, 1, 2, down_y)
     arrive_pair(4)
-    send_pair(4, 12, up_z)
+    send_part(4, 0, 12, up_z)
+    send_part(4, 1, 12, up_z)
     send_pair(4, 6, sibling)
     arrive_pair(5)
-    send_pair(5, 13, down_z)
+    send_part(5, 0, 13, down_z)
+    send_part(5, 1, 13, down_z)
     send_pair(5, 7, sibling)
     for src, base_sem in ((cg, CG), (rg, RG)):
         arrive(src.at[2], base_sem + 2)
@@ -263,12 +279,14 @@
     each(4, 6, whole)
     pl.semaphore_wait(known.at[1], 1)
     tell(known.at[2], up_y, down_y)
-    arrive_pair(12)
-    send_pair(12, 14, sibling)
-    arrive_pair(13)
-    send_pair(13, 15, sibling)
+    for part in range(2):
+        for s in (12, 13):
+            arrive_part(s, part)
+            send_part(s, part, s + 2, sibling)
     each(6, 7, whole)
-    arrive_pair(14, 15)
+    for part in range(2):
+        for s in (14, 15):
+            arrive_part(s, part)
     each(7, 8, whole)
 
     def coupled(k):
@@ -310,6 +328,9 @@
 
     each(0, 8, columns_of)
     own = [coupled(0), coupled(1)]
+    def send_w(s, to, where):
+        send(wb.at[s], wb.at[to], WB + to, where)
+
     for p in range(2):
         near, far = ((3, 4), (2, 5))[p]
         arrive(rs_recv.at[near], RS + near)
@@ -317,24 +338,12 @@
         total = own[p] + rs_recv[near].astype(F32) + rs_recv[far].astype(F32)
         new_t = base[p, 0] - total[0:128] * scale[p]
         new_z = base[p, 1] - total[128:256] * scale[p]
-        new[0, p] = new_t
-        new[1, p] = new_z
+        out_t[p] = new_t
+        out_z[p] = new_z
         product = dot_nt(new_t.astype(BF16), new_z.astype(BF16))
         wb[p] = (0.5 * (product + jnp.transpose(product))).astype(BF16)
-
-    def send_w(s, to, where):
-        send(wb.at[s], wb.at[to], WB + to, where)
-
-    send_w(0, 2, up_z)
-    send_w(1, 3, down_z)
-    send_w(1, 4, up_z)
-    send_w(0, 5, down_z)
-    outs = [
-        pltpu.make_async_copy(new.at[0], out_t, local_sem.at[0]),
-        pltpu.make_async_copy(new.at[1], out_z, local_sem.at[1]),
-    ]
-    for copy in outs:
-        copy.start()
+        send_w(p, (2, 4)[p], up_z)
+        send_w(p, (5, 3)[p], down_z)
     pl.semaphore_wait(known.at[3], 2)
 
     def left_of(*js):
@@ -378,22 +387,18 @@
                     pieces[d * 8 + i].start()
     for copy in sends:
         copy.wait_send()
-    for copy in outs:
-        copy.wait()
     total = obuf[0, x * 2 + c].astype(F32)
     for i in range(1, PIECES):
         pieces[i].wait_recv()
         total = total + rbuf[i].astype(F32)
-    rsum[...] = total
-    last = pltpu.make_async_copy(rsum, out_r, local_sem.at[2])
-    last.start()
+    out_r[...] = total
     for i in range(1, PIECES):
         pieces[i].wait_send()
-    last.wait()
 
 
 def per_device(amps, resp, trans, ints, energies, couple, readers, domains, integrals):
-    anywhere = pl.BlockSpec(memory_space=pl.ANY)
+    anywhere = pl.BlockSpec(memory_space=pltpu.HBM)
+    vmem = pl.BlockSpec(memory_space=pltpu.VMEM)
     dma = pltpu.SemaphoreType.DMA
     return pl.pallas_call(
         kernel,
@@ -403,7 +408,7 @@
             jax.ShapeDtypeStruct((32, 128), F32),
         ),
         in_specs=[anywhere] * 9,
-        out_specs=(anywhere,) * 3,
+        out_specs=(vmem,) * 3,
         scratch_shapes=[
             pltpu.VMEM((16, 768, 128), BF16),
             pltpu.VMEM((8, 512, 128), BF16),
@@ -423,20 +428,23 @@
             pltpu.VMEM((2, 128), F32),
             pltpu.VMEM((2, 2, 128, 128), F32),
             pltpu.VMEM((2, 128, 128), F32),
-            pltpu.VMEM((2, 2, 128, 128), F32),
             pltpu.VMEM((6, 256, 128), BF16),
             pltpu.VMEM((6, 256, 128), BF16),
             pltpu.VMEM((4, 8, 32, 128), BF16),
             pltpu.VMEM((PIECES, 32, 128), BF16),
-            pltpu.VMEM((32, 128), F32),
             dma((16,)), dma((N_SEND,)), dma((N_RECV,)), pltpu.SemaphoreType.REGULAR((4,)),
         ],
         compiler_params=pltpu.CompilerParams(
-            collective_id=0, has_side_effects=True, vmem_limit_bytes=60 * 1024 * 1024
+            collective_id=0, has_side_effects=True, vmem_limit_bytes=32 * 1024 * 1024
         ),
     )(
-        amps, resp, trans, ints, energies, couple, readers, domains.T,
-        integrals.reshape(8, 128, 128),
+        *(
+            pltpu.with_memory_space_constraint(value, pltpu.HBM)
+            for value in (
+                amps, resp, trans, ints, energies, couple, readers, domains.T,
+                integrals.reshape(8, 128, 128),
+            )
+        )
     )
 
 

time: 56.7 us -> 55 us (0.970)
  local copies, waits for them, and re-layouts: 2.93 us -> 1.92 us
  Pallas kernels: 52.9 us -> 52.3 us
    unnamed x7 -> x3, local copies, waits for them, and re-layouts: 2.93 us -> 1.92 us
    pallas_call x1, Pallas kernels: 52.9 us -> 52.3 us  [per_device(): pl.pallas_call(kernel, out_shape=(jax.ShapeDtypeStruct((2, 128, 128), F32...]
where the time goes in v3:
time: 55 us; the launch traced here: 54.9 us
  Pallas kernels  52.3 us (95%)
  local copies, waits for them, and re-layouts  1.92 us (3%)
  between operations  0.64 us (1%)
    pallas_call x1, Pallas kernels, per_device(): pl.pallas_call(kernel, out_shape=(jax.ShapeDtypeStruct((2, 128, 128), F32...  52.3 us
    unnamed x3, local copies, waits for them, and re-layouts  1.92 us

profile of v3, /device:TPU:1, one launch (start us, length us, event | category | flops | bytes accessed | tf_op | source)
XLA Modules:
  0.0 54.9 jit_solution(6619055212767177677)
XLA Ops:
  0.6 52.3 %shard_map.112 = (f32[2,128,128]{2,1,0:T(8,128)S(1)}, f32[2,128,128]{2,1,0:T(8,128)S(1)}, f32[32,128]{1,0:T(8,128)S(1)}) custom-call(bf16[2,128,128]{2,1,0:T(8,128)(2,1)} %amps.1, bf16[2,128,128]{2,1,0:T(8,128)(2,1)} %resp.1, bf16[2,512,128]{2,1,0:T(8,128)(2,1)} %trans.1, bf16[2,128,128]{2,1,0:T(8,128)(2,1)} %ints.1, f32[2,128]{1,0:T(2,128)} %energies.1, ...), custom_call_target="tpu_custom_call" | custom-call | tf_op jit(solution)/shard_map/pallas_call | solution.py:403
  53.0 0.7 %copy.15 = f32[2,128,128]{2,1,0:T(8,128)} copy(f32[2,128,128]{2,1,0:T(8,128)S(1)} %get-tuple-element.6) | data formatting | bytes 262144
  53.6 0.7 %copy.16 = f32[2,128,128]{2,1,0:T(8,128)} copy(f32[2,128,128]{2,1,0:T(8,128)S(1)} %get-tuple-element.7) | data formatting | bytes 262144
  54.3 0.6 %copy.17 = f32[32,128]{1,0:T(8,128)} copy(f32[32,128]{1,0:T(8,128)S(1)} %get-tuple-element.8) | data formatting | bytes 32768

commit v4 on v3

--- a/solution.py
+++ b/solution.py
@@ -292,26 +292,22 @@
     def coupled(k):
         return dot_nt(hall[k], sall[k])
 
-    def pass_on(i, value, where):
-        rs_send[i] = value.astype(BF16)
-        send(rs_send.at[i], rs_recv.at[i], RS + i, where)
-
-    pass_on(0, coupled(6), up_x)
-    pass_on(1, coupled(7), down_x)
-    pass_on(2, coupled(3), up_x)
-    pass_on(3, coupled(2), down_x)
-    part0, part1 = coupled(5), coupled(4)
-    arrive(rs_recv.at[0], RS + 0)
-    pass_on(4, part0 + rs_recv[0].astype(F32), up_x)
-    arrive(rs_recv.at[1], RS + 1)
-    pass_on(5, part1 + rs_recv[1].astype(F32), down_x)
+    for ks in ((6,), (5, 2), (7,), (3, 4)):
+        values = [coupled(k) for k in ks]
+        for k, value in zip(ks, values):
+            dx, p = G_PLACE[k]
+            i = dx * 2 - 2 + p
+            rs_send[i] = value.astype(BF16)
+            send(rs_send.at[i], rs_recv.at[i], RS + i, device(dx=dx))
     pl.semaphore_wait(known.at[2], 2)
     tell(known.at[3], up_y, down_y)
     for d, half in ((3, 1), (1, 0), (2, 0), (2, 1)):
         arrive_x(d, half)
 
     def columns_of(j):
-        s = (j // 2) * 4 + lax.rem(j, 2)
+        p, r = j // 4, lax.rem(j, 4)
+        near = jnp.where(r == 1, 4 + 4 * p, 9 - 4 * p)
+        s = jnp.where(r == 0, p, jnp.where(r == 3, 12 + p, near))
         theirs = domain_of(index_of(s))
         wide_rows = [
             jnp.concatenate([xall[d, theirs[b]] for d in range(RING)], axis=1) for b in range(4)
@@ -332,37 +328,33 @@
         send(wb.at[s], wb.at[to], WB + to, where)
 
     for p in range(2):
-        near, far = ((3, 4), (2, 5))[p]
-        arrive(rs_recv.at[near], RS + near)
-        arrive(rs_recv.at[far], RS + far)
-        total = own[p] + rs_recv[near].astype(F32) + rs_recv[far].astype(F32)
+        total = own[p]
+        for i in (p, 4 + p, 2 + p):
+            arrive(rs_recv.at[i], RS + i)
+            total = total + rs_recv[i].astype(F32)
         new_t = base[p, 0] - total[0:128] * scale[p]
         new_z = base[p, 1] - total[128:256] * scale[p]
         out_t[p] = new_t
         out_z[p] = new_z
         product = dot_nt(new_t.astype(BF16), new_z.astype(BF16))
-        wb[p] = (0.5 * (product + jnp.transpose(product))).astype(BF16)
-        send_w(p, (2, 4)[p], up_z)
-        send_w(p, (5, 3)[p], down_z)
+        wb[p * 4] = (0.5 * (product + jnp.transpose(product))).astype(BF16)
+        send_w(p * 4, p * 4 + 3, device(dz=2))
+        send_w(p * 4, p * 4 + 1, up_z)
+        send_w(p * 4, p * 4 + 2, down_z)
     pl.semaphore_wait(known.at[3], 2)
 
     def left_of(*js):
         for j in js:
             lall[:, j * 128:(j + 1) * 128] = dot(fsel[j], wb[j]).astype(BF16)
 
-    left_of(0, 1)
-    arrive(wb.at[2], WB + 2)
-    send_w(2, 6, up_z)
-    arrive(wb.at[3], WB + 3)
-    send_w(3, 7, down_z)
-    left_of(2, 3)
-    for j in (4, 5):
+    left_of(0, 4)
+    for j in (1, 2, 3):
         arrive(wb.at[j], WB + j)
-    left_of(4, 5)
-    early = dot(lall[:, 0:768], yall[0:768, :])
-    for j in (6, 7):
+    left_of(1, 2, 3)
+    early = dot(lall[:, 0:512], yall[0:512, :])
+    for j in (5, 6, 7):
         arrive(wb.at[j], WB + j)
-    left_of(6, 7)
+    left_of(5, 6, 7)
 
     def piece(i):
         dy, dx, dc = i // 8, (i // 2) % 4, i % 2
@@ -376,7 +368,7 @@
     pieces = [None] + [piece(i) for i in range(1, PIECES)]
     for dys in ((2, 3), (0, 1)):
         columns = slice(dys[0] * 128, dys[0] * 128 + 256)
-        partial = early[:, columns] + dot(lall[:, 768:1024], yall[768:1024, columns])
+        partial = early[:, columns] + dot(lall[:, 512:1024], yall[512:1024, columns])
         for d in dys:
             for i in range(8):
                 block = partial[i * 32:(i + 1) * 32, (d - dys[0]) * 128:(d - dys[0] + 1) * 128]

time: 55 us -> 52.5 us (0.955)
  Pallas kernels: 52.3 us -> 49.8 us
    pallas_call x1, Pallas kernels: 52.3 us -> 49.8 us  [per_device(): pl.pallas_call(kernel, out_shape=(jax.ShapeDtypeStruct((2, 128, 128), F32...]
where the time goes in v4:
time: 52.5 us; the launch traced here: 52.4 us
  Pallas kernels  49.8 us (95%)
  local copies, waits for them, and re-layouts  1.92 us (4%)
  between operations  0.64 us (1%)
    pallas_call x1, Pallas kernels, per_device(): pl.pallas_call(kernel, out_shape=(jax.ShapeDtypeStruct((2, 128, 128), F32...  49.8 us
    unnamed x3, local copies, waits for them, and re-layouts  1.92 us

profile of v4, /device:TPU:1, one launch (start us, length us, event | category | flops | bytes accessed | tf_op | source)
XLA Modules:
  0.0 52.4 jit_solution(11651588786571200103)
XLA Ops:
  0.6 49.8 %shard_map.112 = (f32[2,128,128]{2,1,0:T(8,128)S(1)}, f32[2,128,128]{2,1,0:T(8,128)S(1)}, f32[32,128]{1,0:T(8,128)S(1)}) custom-call(bf16[2,128,128]{2,1,0:T(8,128)(2,1)} %amps.1, bf16[2,128,128]{2,1,0:T(8,128)(2,1)} %resp.1, bf16[2,512,128]{2,1,0:T(8,128)(2,1)} %trans.1, bf16[2,128,128]{2,1,0:T(8,128)(2,1)} %ints.1, f32[2,128]{1,0:T(2,128)} %energies.1, ...), custom_call_target="tpu_custom_call" | custom-call | tf_op jit(solution)/shard_map/pallas_call | solution.py:395
  50.5 0.7 %copy.15 = f32[2,128,128]{2,1,0:T(8,128)} copy(f32[2,128,128]{2,1,0:T(8,128)S(1)} %get-tuple-element.6) | data formatting | bytes 262144
  51.1 0.7 %copy.16 = f32[2,128,128]{2,1,0:T(8,128)} copy(f32[2,128,128]{2,1,0:T(8,128)S(1)} %get-tuple-element.7) | data formatting | bytes 262144
  51.8 0.6 %copy.17 = f32[32,128]{1,0:T(8,128)} copy(f32[32,128]{1,0:T(8,128)S(1)} %get-tuple-element.8) | data formatting | bytes 32768

commit v5 on v4

--- a/solution.py
+++ b/solution.py
@@ -40,7 +40,7 @@
 
 def kernel(
     amps, resp, trans, ints, energies, couple, readers, domains, integrals,
-    out_t, out_z, out_r,
+    out,
     hb, qg, at, sall, hall, xall, yall, fsel, lall, wb, coef, cg, rg, dom, ex, en,
     base, scale, rs_send, rs_recv, obuf, rbuf,
     local_sem, send_sem, recv_sem, known,
@@ -136,6 +136,9 @@
         send(amps.at[p], hb.at[to, 512:640], HB + to, where)
         send(resp.at[p], hb.at[to, 640:768], HB + to, where)
 
+    for src, dst, base_sem in ((couple, cg, CG), (readers, rg, RG)):
+        send(src, dst.at[3], base_sem + 3, up_x)
+        send(src, dst.at[1], base_sem + 1, down_x)
     send_own(0, 4, up_z)
     send_own(1, 5, down_z)
     send_g(trans.at[0], 2, up_x)
@@ -146,9 +149,6 @@
     send_own(0, 9, down_z)
     send_g(trans.at[1], 4, up_x)
     send_g(trans.at[0], 5, down_x)
-    for src, dst, base_sem in ((couple, cg, CG), (readers, rg, RG)):
-        send(src, dst.at[3], base_sem + 3, up_x)
-        send(src, dst.at[1], base_sem + 1, down_x)
     for half, to, where in ((0, 3, up_y), (1, 1, down_y), (1, 3, up_y), (0, 1, down_y)):
         rows = slice(half * 4, half * 4 + 4)
         send(integrals.at[rows], xall.at[to, rows], XA + to * 2 + half, where)
@@ -186,18 +186,18 @@
         zz, cc, pair = place(s)
         return (((zz * RING + x) * 2 + cc) * RING + y) * 2 + pair
 
-    def tile(i, low):
+    def tile(i, low, size=HALF):
         pair = (2 * i, 2 * i + 1)
         inters = []
         for s in pair:
             theirs = domain_of(index_of(s))
-            left = jnp.concatenate([at[theirs[b], low:low + HALF, :] for b in range(4)], axis=1)
+            left = jnp.concatenate([at[theirs[b], low:low + size, :] for b in range(4)], axis=1)
             inters.append(dot(left, hb[s, 0:512, :]).astype(BF16))
         for s, inter in zip(pair, inters):
             columns = pl.ds(pl.multiple_of(s * 128, 128), 128)
             both = jnp.concatenate([hb[s, 512:640, :], hb[s, 640:768, :]], axis=1)
             half = dot(inter, both)
-            for j in range(HALF // 128):
+            for j in range(size // 128):
                 k = low // 128 + j
                 rows = slice(j * 128, (j + 1) * 128)
                 weight = coef[k, pl.ds(s, 1), :]
@@ -260,6 +260,7 @@
     build_at(5)
     arrive_pair(6, 7)
     each(2, 4, lambda i: tile(i, 0))
+    each(0, 4, lambda i: tile(i, HALF, HALF // 2))
     pl.semaphore_wait(known.at[0], 2)
     tell(known.at[1], sibling)
     arrive_g(6, 7)
@@ -269,7 +270,7 @@
     send_pair(8, 10, sibling)
     arrive_pair(9)
     send_pair(9, 11, sibling)
-    each(0, 4, lambda i: tile(i, HALF))
+    each(0, 4, lambda i: tile(i, HALF + HALF // 2, HALF // 2))
     arrive_pair(10, 11)
 
     def whole(i):
@@ -322,20 +323,19 @@
                 )
             fsel[j, i * 128:(i + 1) * 128, :] = value
 
-    each(0, 8, columns_of)
-    own = [coupled(0), coupled(1)]
+    each(0, 4, columns_of)
     def send_w(s, to, where):
         send(wb.at[s], wb.at[to], WB + to, where)
 
     for p in range(2):
-        total = own[p]
+        total = coupled(p)
         for i in (p, 4 + p, 2 + p):
             arrive(rs_recv.at[i], RS + i)
             total = total + rs_recv[i].astype(F32)
         new_t = base[p, 0] - total[0:128] * scale[p]
         new_z = base[p, 1] - total[128:256] * scale[p]
-        out_t[p] = new_t
-        out_z[p] = new_z
+        out[p * 128:(p + 1) * 128] = new_t
+        out[256 + p * 128:384 + p * 128] = new_z
         product = dot_nt(new_t.astype(BF16), new_z.astype(BF16))
         wb[p * 4] = (0.5 * (product + jnp.transpose(product))).astype(BF16)
         send_w(p * 4, p * 4 + 3, device(dz=2))
@@ -347,6 +347,7 @@
         for j in js:
             lall[:, j * 128:(j + 1) * 128] = dot(fsel[j], wb[j]).astype(BF16)
 
+    each(4, 8, columns_of)
     left_of(0, 4)
     for j in (1, 2, 3):
         arrive(wb.at[j], WB + j)
@@ -383,7 +384,7 @@
     for i in range(1, PIECES):
         pieces[i].wait_recv()
         total = total + rbuf[i].astype(F32)
-    out_r[...] = total
+    out[512:544] = total
     for i in range(1, PIECES):
         pieces[i].wait_send()
 
@@ -392,15 +393,11 @@
     anywhere = pl.BlockSpec(memory_space=pltpu.HBM)
     vmem = pl.BlockSpec(memory_space=pltpu.VMEM)
     dma = pltpu.SemaphoreType.DMA
-    return pl.pallas_call(
+    out = pl.pallas_call(
         kernel,
-        out_shape=(
-            jax.ShapeDtypeStruct((2, 128, 128), F32),
-            jax.ShapeDtypeStruct((2, 128, 128), F32),
-            jax.ShapeDtypeStruct((32, 128), F32),
-        ),
+        out_shape=jax.ShapeDtypeStruct((544, 128), F32),
         in_specs=[anywhere] * 9,
-        out_specs=(vmem,) * 3,
+        out_specs=vmem,
         scratch_shapes=[
             pltpu.VMEM((16, 768, 128), BF16),
             pltpu.VMEM((8, 512, 128), BF16),
@@ -438,6 +435,9 @@
             )
         )
     )
+    return (
+        out[0:256].reshape(2, 128, 128), out[256:512].reshape(2, 128, 128), out[512:544],
+    )
 
 
 def solution(mesh):

time: 52.5 us -> 50.5 us (0.962)
  Pallas kernels: 49.8 us -> 48.4 us
  local copies, waits for them, and re-layouts: 1.92 us -> 1.32 us
    unnamed x3 -> x0, local copies, waits for them, and re-layouts: 1.92 us -> none
    pallas_call x1, Pallas kernels: 49.8 us -> 48.4 us  [per_device(): pl.pallas_call(kernel, out_shape=jax.ShapeDtypeStruct((544, 128), F32), i...]
    slice x0 -> x2, local copies, waits for them, and re-layouts: none -> 1.32 us  [the longest x1 0.72 us: per_device(): out[256:512].reshape(2, 128, 128)]
where the time goes in v5:
time: 50.5 us; the launch traced here: 50.4 us
  Pallas kernels  48.4 us (96%)
  local copies, waits for them, and re-layouts  1.32 us (3%)
  between operations  0.64 us (1%)
    pallas_call x1, Pallas kernels, per_device(): pl.pallas_call(kernel, out_shape=jax.ShapeDtypeStruct((544, 128), F32), i...  48.4 us

profile of v5, /device:TPU:1, one launch (start us, length us, event | category | flops | bytes accessed | tf_op | source)
XLA Modules:
  0.0 50.4 jit_solution(1865566988556341644)
XLA Ops:
  0.6 48.4 %shard_map.112 = f32[544,128]{1,0:T(8,128)S(1)} custom-call(bf16[2,128,128]{2,1,0:T(8,128)(2,1)} %amps.1, bf16[2,128,128]{2,1,0:T(8,128)(2,1)} %resp.1, bf16[2,512,128]{2,1,0:T(8,128)(2,1)} %trans.1, bf16[2,128,128]{2,1,0:T(8,128)(2,1)} %ints.1, f32[2,128]{1,0:T(2,128)} %energies.1, f32[2,48]{1,0:T(2,128)} %couple.1, s32[2,48]{1,0:T(2,128)} %readers.1, ...), custom_call_target="tpu_custom_call" | custom-call | tf_op jit(solution)/shard_map/pallas_call | solution.py:396
  49.0 0.7 %fusion = (f32[256,128]{1,0:T(8,128)}, f32[256,128]{1,0:T(8,128)}) fusion(f32[544,128]{1,0:T(8,128)S(1)} %shard_map.112), kind=kLoop, calls=%fused_computation | loop fusion | bytes 524288 | tf_op jit(solution)/shard_map/slice | solution.py:439
  49.8 0.6 %slice.11 = f32[32,128]{1,0:T(8,128)} slice(f32[544,128]{1,0:T(8,128)S(1)} %shard_map.112), slice={[512:544], [0:128]} | slice | bytes 32768 | tf_op jit(solution)/shard_map/slice | solution.py:439

commit v6 on v5

--- a/solution.py
+++ b/solution.py
@@ -271,19 +271,22 @@
     arrive_pair(9)
     send_pair(9, 11, sibling)
     each(0, 4, lambda i: tile(i, HALF + HALF // 2, HALF // 2))
-    arrive_pair(10, 11)
+    def hand_on(part):
+        for s in (12, 13):
+            arrive_part(s, part)
+            send_part(s, part, s + 2, sibling)
 
     def whole(i):
         tile(i, 0)
         tile(i, HALF)
 
-    each(4, 6, whole)
+    each(4, 5, whole)
+    hand_on(0)
+    arrive_pair(10, 11)
+    each(5, 6, whole)
+    hand_on(1)
     pl.semaphore_wait(known.at[1], 1)
     tell(known.at[2], up_y, down_y)
-    for part in range(2):
-        for s in (12, 13):
-            arrive_part(s, part)
-            send_part(s, part, s + 2, sibling)
     each(6, 7, whole)
     for part in range(2):
         for s in (14, 15):

time: 50.5 us -> 49.8 us (0.986)
  Pallas kernels: 48.4 us -> 47.8 us
    pallas_call x1, Pallas kernels: 48.4 us -> 47.8 us  [per_device(): pl.pallas_call(kernel, out_shape=jax.ShapeDtypeStruct((544, 128), F32), i...]
where the time goes in v6:
time: 49.8 us; the launch traced here: 49.7 us
  Pallas kernels  47.8 us (96%)
  local copies, waits for them, and re-layouts  1.32 us (3%)
  between operations  0.64 us (1%)
    pallas_call x1, Pallas kernels, per_device(): pl.pallas_call(kernel, out_shape=jax.ShapeDtypeStruct((544, 128), F32), i...  47.8 us

profile of v6, /device:TPU:1, one launch (start us, length us, event | category | flops | bytes accessed | tf_op | source)
XLA Modules:
  0.0 49.7 jit_solution(16260761246746682272)
XLA Ops:
  0.6 47.8 %shard_map.112 = f32[544,128]{1,0:T(8,128)S(1)} custom-call(bf16[2,128,128]{2,1,0:T(8,128)(2,1)} %amps.1, bf16[2,128,128]{2,1,0:T(8,128)(2,1)} %resp.1, bf16[2,512,128]{2,1,0:T(8,128)(2,1)} %trans.1, bf16[2,128,128]{2,1,0:T(8,128)(2,1)} %ints.1, f32[2,128]{1,0:T(2,128)} %energies.1, f32[2,48]{1,0:T(2,128)} %couple.1, s32[2,48]{1,0:T(2,128)} %readers.1, ...), custom_call_target="tpu_custom_call" | custom-call | tf_op jit(solution)/shard_map/pallas_call | solution.py:399
  48.4 0.7 %fusion = (f32[256,128]{1,0:T(8,128)}, f32[256,128]{1,0:T(8,128)}) fusion(f32[544,128]{1,0:T(8,128)S(1)} %shard_map.112), kind=kLoop, calls=%fused_computation | loop fusion | bytes 524288 | tf_op jit(solution)/shard_map/slice | solution.py:442
  49.1 0.6 %slice.11 = f32[32,128]{1,0:T(8,128)} slice(f32[544,128]{1,0:T(8,128)S(1)} %shard_map.112), slice={[512:544], [0:128]} | slice | bytes 32768 | tf_op jit(solution)/shard_map/slice | solution.py:442
